TPU v7x, 32 devices: a whole 2x2x4 slice. The times are simulated.
32 devices in a mesh: row: 8 (over z, y), col: 4 (over x, core).
Axes of the slice: x: 2, y: 2, z: 4, core: 2. Of those that a mesh axis runs over, the one named last changes fastest.
Arguments:
- matrix: bfloat16 [12, 8, 256, 24, 4, 256], P(None, 'row', None, None, 'col'), as said below
- inv_first: bfloat16 [512, 512], replicated, as said below
- inv_second: bfloat16 [512, 512], replicated, as said below
Outputs:
- panels: bfloat16 [12, 8, 256, 1024], P(None, 'row')
- trailing: bfloat16 [12, 8, 256, 24, 4, 256], P(None, 'row', None, None, 'col')
Inputs may be any that keep to these rules, and one draw needn't show every extreme that they name: `matrix`: symmetric: the entry at (i, j) of M equals the entry at (j, i). `inv_first`: lower triangular: entries above the diagonal are zero, diagonal entries are positive. `inv_second`: lower triangular: entries above the diagonal are zero, diagonal entries are positive.
All inputs are finite; a program needn't handle non-finite values.
Results may differ from a plain program's by a relative error of at most 0.0065.
Values may be sent and summed in bfloat16 or wider, within the bound.
No kernel may reach another device: no remote copies, remote signals or barrier semaphores. Data moves between devices by JAX's collectives and lax.ppermute only.
A program may use at most 256 MiB of HBM per device.

v0:
```python
import jax
import jax.numpy as jnp
from jax import lax
from jax.sharding import PartitionSpec as P


def from_root(value, axis, source):
    kept = jnp.where(lax.axis_index(axis) == source, value, 0).astype(value.dtype)
    return lax.psum(kept, axis)


def outer_minus(target, left_rows, right_rows):
    product = lax.dot_general(
        left_rows, right_rows, (((1,), (1,)), ((), ())), preferred_element_type=jnp.float32
    )
    return (target.astype(jnp.float32) - product).astype(jnp.bfloat16)


def panel_columns(first_tile, step_index):
    halves = []
    for half_index in range(2):
        halves.append(from_root(first_tile, "col", 2 * step_index + half_index))
    return jnp.concatenate(halves, axis=1)


def column_factor(row_factor, col_id, row_count, col_count):
    owner_count = row_count // col_count
    received = []
    for owner_slot in range(owner_count):
        received.append(from_root(row_factor, "row", owner_slot * col_count + col_id))
    gathered = jnp.stack(received, axis=1)
    return gathered.reshape(-1, gathered.shape[-1])


def local(matrix, inv_first, inv_second):
    row_count = lax.axis_size("row")
    col_count = lax.axis_size("col")
    row_id = lax.axis_index("row")
    col_id = lax.axis_index("col")
    tile_rows = matrix.shape[0]
    tile_size = matrix.shape[2]
    tile_cols = matrix.shape[3]
    width = inv_first.shape[0]
    local_rows = tile_rows * tile_size
    local_cols = tile_cols * tile_size
    current = matrix.reshape(local_rows, local_cols)
    row_position = jnp.arange(local_rows, dtype=jnp.int32)
    global_rows = (
        row_position // tile_size * row_count + row_id
    ) * tile_size + row_position % tile_size
    col_position = jnp.arange(local_cols, dtype=jnp.int32)
    global_cols = (
        col_position // tile_size * col_count + col_id
    ) * tile_size + col_position % tile_size

    def factor_rows(first_tile, inverse, step_index):
        columns = panel_columns(first_tile, step_index)
        product = lax.dot_general(
            columns, inverse, (((1,), (1,)), ((), ())), preferred_element_type=jnp.float32
        )
        keep_rows = (global_rows >= (step_index + 1) * width)[:, None]
        return jnp.where(keep_rows, product, jnp.zeros_like(product)).astype(jnp.bfloat16)

    def spread_columns(row_factor):
        shaped = row_factor.reshape(tile_rows, tile_size, width)
        return column_factor(shaped, col_id, row_count, col_count)

    row_first = factor_rows(current[:, :tile_size], inv_first, 0)
    col_first = spread_columns(row_first)
    updated = outer_minus(current, row_first, col_first)
    row_second = factor_rows(updated[:, :tile_size], inv_second, 1)
    col_second = spread_columns(row_second)
    result = outer_minus(updated, row_second, col_second)
    row_tiles = global_rows // tile_size
    col_tiles = global_cols // tile_size
    keep_mask = (
        (global_rows >= 2 * width)[:, None]
        & (global_cols >= 2 * width)[None, :]
        & (row_tiles[:, None] >= col_tiles[None, :])
    )
    trailing = jnp.where(keep_mask, result, jnp.zeros_like(result))
    panels = jnp.concatenate([row_first, row_second], axis=1)
    return (panels.reshape(tile_rows, 1, tile_size, 2 * width), trailing.reshape(matrix.shape))


def solution(mesh):
    placed = (P(None, "row", None, None, "col", None), P(), P())
    return jax.shard_map(
        local,
        mesh=mesh,
        in_specs=placed,
        out_specs=(P(None, "row", None, None), P(None, "row", None, None, "col", None)),
        check_vma=False,
    )
```

profile of v0, /device:TPU:0, one launch (start us, length us, event | category | flops | bytes accessed | tf_op | source)
XLA Modules:
  0.0 727.5 jit_solution(10933837619219839394)
XLA Ops:
  7.2 0.0 all-reduce.15.cloned.1.call-start
  7.2 26.1 %copy.13 = bf16[384,8,24,256]{3,1,2,0:T(8,128)(2,1)} copy(bf16[384,8,24,256]{3,2,1,0:T(8,128)(2,1)} %bitcast.35) | data formatting | bytes 75497472
  33.3 3.3 broadcast_select_fusion.7
  36.6 0.0 all-reduce.15.cloned.1.call-update
  36.6 0.0 all-reduce.11.cloned.1.call-start
  36.7 71.4 %all-reduce.15.cloned.1.call-done = (bf16[3072,256]{1,0:T(8,128)(2,1)}, bf16[3072,256]{1,0:T(8,128)(2,1)}) async-done(((bf16[3072,256]{1,0:T(8,128)(2,1)}, bf16[3072,256]{1,0:T(8,128)(2,1)}), (bf16[3072,256]{1,0:T(8,128)(2,1)}, bf16[3072,256]{1,0:T(8,128)(2,1)})) %all-reduce.15.cloned.1.call-update) | async-done | bytes 3145744 | tf_op jit(solution)/shard_map/psum | solution.py:9
  108.1 6.4 broadcast_select_fusion.3
  114.5 0.0 all-reduce.11.cloned.1.call-update
  114.5 0.0 all-reduce.13.cloned.1.call-start
  114.6 212.7 %all-reduce.11.cloned.1.call-done = (bf16[12,1,256,512]{3,2,1,0:T(8,128)(2,1)}, bf16[12,1,256,512]{3,2,1,0:T(8,128)(2,1)}) async-done(((bf16[12,1,256,512]{3,2,1,0:T(8,128)(2,1)}, bf16[12,1,256,512]{3,2,1,0:T(8,128)(2,1)}), (bf16[12,1,256,512]{3,2,1,0:T(8,128)(2,1)}, bf16[12,1,256,512]{3,2,1,0:T(8,128)(2,1)})) %all-reduce.11.cloned.1.call-update) | async-done | bytes 6291472 | tf_op jit(solution)/shard_map/psum | solution.py:9
  327.2 3.6 pad_maximum_fusion
  330.8 0.2 copy-done.2
  331.0 32.4 %subtract_convert_fusion.1 = bf16[3072,6144]{1,0:T(8,128)(2,1)} fusion(bf16[3072,6144]{1,0:T(8,128)(2,1)} %bitcast.34, bf16[3072,512]{1,0:T(8,128)(2,1)S(1)} %copy-done.2, bf16[6144,512]{1,0:T(8,128)(2,1)S(1)} %bitcast.40), kind=kOutput, calls=%fused_computation.1 | convolution fusion | flops 19383975936 | bytes 84934656 | tf_op jit(solution)/shard_map/dot_general | solution.py:13
  363.4 3.3 broadcast_select_fusion.5
  366.7 0.0 all-reduce.13.cloned.1.call-update
  366.8 0.2 all-reduce.9.cloned.1.call-start
  367.0 67.5 %all-reduce.13.cloned.1.call-done = (bf16[3072,256]{1,0:T(8,128)(2,1)}, bf16[3072,256]{1,0:T(8,128)(2,1)}) async-done(((bf16[3072,256]{1,0:T(8,128)(2,1)}, bf16[3072,256]{1,0:T(8,128)(2,1)}), (bf16[3072,256]{1,0:T(8,128)(2,1)}, bf16[3072,256]{1,0:T(8,128)(2,1)})) %all-reduce.13.cloned.1.call-update) | async-done | bytes 3145744 | tf_op jit(solution)/shard_map/psum | solution.py:9
  434.6 6.3 broadcast_select_fusion.2
  440.9 0.0 all-reduce.9.cloned.1.call-update
  441.0 6.6 pad_maximum_fusion.1
  447.6 206.1 %all-reduce.9.cloned.1.call-done = (bf16[12,1,256,512]{3,2,1,0:T(8,128)(2,1)}, bf16[12,1,256,512]{3,2,1,0:T(8,128)(2,1)}) async-done(((bf16[12,1,256,512]{3,2,1,0:T(8,128)(2,1)}, bf16[12,1,256,512]{3,2,1,0:T(8,128)(2,1)}), (bf16[12,1,256,512]{3,2,1,0:T(8,128)(2,1)}, bf16[12,1,256,512]{3,2,1,0:T(8,128)(2,1)})) %all-reduce.9.cloned.1.call-update) | async-done | bytes 6291472 | tf_op jit(solution)/shard_map/psum | solution.py:9
  653.6 6.1 pad_maximum_fusion.2
  659.7 35.9 %and_select_fusion = bf16[3072,6144]{1,0:T(8,128)(2,1)} fusion(bf16[3072,6144]{1,0:T(8,128)(2,1)} %subtract_convert_fusion.1, s32[6144]{0:T(1024)S(1)} %add_select_fusion, s32[3072]{0:T(1024)S(1)} %add_select_fusion.2, pred[6144]{0:T(1024)(128)(4,1)S(1)} %broadcast_compare_fusion, pred[3072]{0:T(1024)(128)(4,1)S(1)} %broadcast_compare_fusion.1, ...), kind=kOutput, calls=%fused_computation.2 | convolution fusion | flops 19459473408 | bytes 84980736 | tf_op jit(solution)/shard_map/dot_general | solution.py:13
  695.5 25.5 %copy.14 = bf16[384,8,24,256]{3,2,1,0:T(8,128)(2,1)} copy(bf16[384,8,24,256]{3,1,2,0:T(8,128)(2,1)} %bitcast.36) | data formatting | bytes 75497472
  (12 shorter events, 0.1 us)
Async XLA Ops:
  7.2 101.0 %copy-start = (bf16[512,512]{1,0:T(8,128)(2,1)S(1)}, bf16[512,512]{1,0:T(8,128)(2,1)}, u32[]{:S(2)}) copy-start(bf16[512,512]{1,0:T(8,128)(2,1)} %param.4) | copy-start | bytes 1572868
  7.2 100.9 %all-reduce.15.cloned.1.call-start = ((), (), s32[]{:S(2)}) async-start(), calls=%async_computation.3 | async-start | bytes 6291456 | tf_op jit(solution)/shard_map/psum | solution.py:9
  36.6 290.6 %all-reduce.11.cloned.1.call-start = ((), (), s32[]{:S(2)}) async-start(), calls=%async_computation.1 | async-start | bytes 12582912 | tf_op jit(solution)/shard_map/psum | solution.py:9
  114.5 320.0 %all-reduce.13.cloned.1.call-start = ((), (), s32[]{:S(2)}) async-start(), calls=%async_computation.2 | async-start | bytes 6291456 | tf_op jit(solution)/shard_map/psum | solution.py:9
  327.2 3.7 copy-start.2
  363.4 71.2 %copy-start.3 = (bf16[512,512]{1,0:T(8,128)(2,1)S(1)}, bf16[512,512]{1,0:T(8,128)(2,1)}, u32[]{:S(2)}) copy-start(bf16[512,512]{1,0:T(8,128)(2,1)} %param.5) | copy-start | bytes 1572868
  366.8 286.8 %all-reduce.9.cloned.1.call-start = ((), (), s32[]{:S(2)}) async-start(), calls=%async_computation | async-start | bytes 12582912 | tf_op jit(solution)/shard_map/psum | solution.py:9
  695.5 25.5 %copy-start.1 = (bf16[512,512]{1,0:T(8,128)(2,1)S(1)}, bf16[512,512]{1,0:T(8,128)(2,1)}, u32[]{:S(2)}) copy-start(bf16[512,512]{1,0:T(8,128)(2,1)} %param.4) | copy-start | bytes 1572868
Sparse Core Ops, SparseCore 0:
  36.8 71.3 all-reduce.14
  114.7 212.5 all-reduce.10
  366.9 67.6 all-reduce.12
  441.0 212.5 all-reduce.8
where the time goes:
time: 728 us
  waiting for transfers between devices  558 us (77%)
  matrix products  81 us (11%)
  local copies, waits for them, and re-layouts  51.7 us (7%)
  other arithmetic  22.9 us (3%)
  between operations  13.9 us (2%)
    psum x4, waiting for transfers between devices, from_root(): return lax.psum(kept, axis)  558 us
    dot_general x2, matrix products, outer_minus(): lax.dot_general(left_rows, right_rows, (((1,), (1,)), ((), ())), preferre...  68.3 us
    unnamed x10, local copies, waits for them, and re-layouts  51.7 us
  transfers between devices with their start and end apart: 4, of which 4 were waited for; matrix products, arithmetic and copies ran while one was open for 1% of the time, Pallas kernels for 0%

commit v1 on v0

--- a/solution.py
+++ b/solution.py
@@ -6,7 +6,7 @@
 
 def from_root(value, axis, source):
     kept = jnp.where(lax.axis_index(axis) == source, value, 0).astype(value.dtype)
-    return lax.psum(kept, axis)
+    return jnp.sum(lax.all_gather(kept, axis), axis=0)
 
 
 def outer_minus(target, left_rows, right_rows):

time: 728 us -> 2320 us (3.19)
  waiting for transfers between devices: 558 us -> 2070 us
  other arithmetic: 22.9 us -> 105 us
    all_gather x0 -> x8, waiting for transfers between devices: none -> 2070 us  [from_root(): return jnp.sum(lax.all_gather(kept, axis), axis=0)]
    psum x4 -> x0, waiting for transfers between devices: 558 us -> none  [from_root(): return lax.psum(kept, axis)]
    reduce_sum x0 -> x8, other arithmetic: none -> 81.8 us  [from_root(): return jnp.sum(lax.all_gather(kept, axis), axis=0)]
  transfers between devices with their start and end apart: 4 -> 8, of which waited for: 4 -> 8; matrix products, arithmetic and copies ran while one was open for 1% -> 2% of each run, Pallas kernels for 0% -> 0%
where the time goes in v1:
time: 2320 us
  waiting for transfers between devices  2070 us (89%)
  other arithmetic  105 us (5%)
  matrix products  80.4 us (3%)
  local copies, waits for them, and re-layouts  51.7 us (2%)
    all_gather x8, waiting for transfers between devices, from_root(): return jnp.sum(lax.all_gather(kept, axis), axis=0)  2070 us
    reduce_sum x8, other arithmetic, from_root(): return jnp.sum(lax.all_gather(kept, axis), axis=0)  81.8 us
    dot_general x2, matrix products, outer_minus(): lax.dot_general(left_rows, right_rows, (((1,), (1,)), ((), ())), preferre...  68.3 us
    unnamed x10, local copies, waits for them, and re-layouts  51.7 us
  transfers between devices with their start and end apart: 8, of which 8 were waited for; matrix products, arithmetic and copies ran while one was open for 2% of the time, Pallas kernels for 0%

profile of v1, /device:TPU:0, one launch (start us, length us, event | category | flops | bytes accessed | tf_op | source)
XLA Modules:
  0.0 2320.2 jit_solution(487117272088322419)
XLA Ops:
  7.2 26.1 %copy.11 = bf16[384,8,24,256]{3,1,2,0:T(8,128)(2,1)} copy(bf16[384,8,24,256]{3,2,1,0:T(8,128)(2,1)} %bitcast.35) | data formatting | bytes 75497472
  37.5 48.4 %all-gather.21.cloned.1.call-done = bf16[12288,256]{1,0:T(8,128)(2,1)} async-done(((bf16[3072,256]{1,0:T(8,128)(2,1)}), bf16[12288,256]{1,0:T(8,128)(2,1)}) %all-gather.21.cloned.1.call-update) | async-done | bytes 6291472 | tf_op jit(solution)/shard_map/all_gather | solution.py:9
  85.9 4.8 reduce_sum.96
  90.6 43.2 %all-gather.23.cloned.1.call-done = bf16[12288,256]{1,0:T(8,128)(2,1)} async-done(((bf16[3072,256]{1,0:T(8,128)(2,1)}), bf16[12288,256]{1,0:T(8,128)(2,1)}) %all-gather.23.cloned.1.call-update) | async-done | bytes 6291472 | tf_op jit(solution)/shard_map/all_gather | solution.py:9
  133.8 5.3 reduce_sum.97
  139.1 6.1 broadcast_select_fusion.3
  146.1 479.8 %all-gather.13.cloned.1.call-done = bf16[8,12,256,512]{3,2,1,0:T(8,128)(2,1)} async-done(((bf16[1,12,256,512]{3,2,1,0:T(8,128)(2,1)}), bf16[8,12,256,512]{3,2,1,0:T(8,128)(2,1)}) %all-gather.13.cloned.1.call-update) | async-done | bytes 25165840 | tf_op jit(solution)/shard_map/all_gather | solution.py:9
  625.8 15.6 reduce_sum.98
  641.4 466.2 %all-gather.15.cloned.1.call-done = bf16[8,12,256,512]{3,2,1,0:T(8,128)(2,1)} async-done(((bf16[1,12,256,512]{3,2,1,0:T(8,128)(2,1)}), bf16[8,12,256,512]{3,2,1,0:T(8,128)(2,1)}) %all-gather.15.cloned.1.call-update) | async-done | bytes 25165840 | tf_op jit(solution)/shard_map/all_gather | solution.py:9
  1107.7 15.2 reduce_sum.99
  1126.7 32.4 %subtract_convert_fusion.1 = bf16[3072,6144]{1,0:T(8,128)(2,1)} fusion(bf16[3072,6144]{1,0:T(8,128)(2,1)} %bitcast.34, bf16[3072,512]{1,0:T(8,128)(2,1)S(1)} %copy-done.2, bf16[6144,512]{1,0:T(8,128)(2,1)S(1)} %bitcast.44), kind=kOutput, calls=%fused_computation.1 | convolution fusion | flops 19383975936 | bytes 84934656 | tf_op jit(solution)/shard_map/dot_general | solution.py:13
  1163.0 45.9 %all-gather.25.cloned.1.call-done = bf16[12288,256]{1,0:T(8,128)(2,1)} async-done(((bf16[3072,256]{1,0:T(8,128)(2,1)}), bf16[12288,256]{1,0:T(8,128)(2,1)}) %all-gather.25.cloned.1.call-update) | async-done | bytes 6291472 | tf_op jit(solution)/shard_map/all_gather | solution.py:9
  1208.9 4.8 reduce_sum.100
  1213.6 43.1 %all-gather.27.cloned.1.call-done = bf16[12288,256]{1,0:T(8,128)(2,1)} async-done(((bf16[3072,256]{1,0:T(8,128)(2,1)}), bf16[12288,256]{1,0:T(8,128)(2,1)}) %all-gather.27.cloned.1.call-update) | async-done | bytes 6291472 | tf_op jit(solution)/shard_map/all_gather | solution.py:9
  1256.7 5.3 reduce_sum.101
  1262.0 6.0 broadcast_select_fusion.2
  1268.9 6.4 pad_maximum_fusion.1
  1275.3 473.3 %all-gather.17.cloned.1.call-done = bf16[8,12,256,512]{3,2,1,0:T(8,128)(2,1)} async-done(((bf16[1,12,256,512]{3,2,1,0:T(8,128)(2,1)}), bf16[8,12,256,512]{3,2,1,0:T(8,128)(2,1)}) %all-gather.17.cloned.1.call-update) | async-done | bytes 25165840 | tf_op jit(solution)/shard_map/all_gather | solution.py:9
  1748.7 15.6 reduce_sum.102
  1764.2 466.4 %all-gather.19.cloned.1.call-done = bf16[8,12,256,512]{3,2,1,0:T(8,128)(2,1)} async-done(((bf16[1,12,256,512]{3,2,1,0:T(8,128)(2,1)}), bf16[8,12,256,512]{3,2,1,0:T(8,128)(2,1)}) %all-gather.19.cloned.1.call-update) | async-done | bytes 25165840 | tf_op jit(solution)/shard_map/all_gather | solution.py:9
  2230.6 15.3 reduce_sum.103
  2245.9 6.1 pad_maximum_fusion.2
  2252.0 35.9 %and_select_fusion = bf16[3072,6144]{1,0:T(8,128)(2,1)} fusion(bf16[3072,6144]{1,0:T(8,128)(2,1)} %subtract_convert_fusion.1, s32[6144]{0:T(1024)S(1)} %add_select_fusion, s32[3072]{0:T(1024)S(1)} %add_select_fusion.2, pred[6144]{0:T(1024)(128)(4,1)S(1)} %broadcast_compare_fusion, pred[3072]{0:T(1024)(128)(4,1)S(1)} %broadcast_compare_fusion.1, ...), kind=kOutput, calls=%fused_computation.2 | convolution fusion | flops 19459473408 | bytes 84980736 | tf_op jit(solution)/shard_map/dot_general | solution.py:13
  2287.9 25.5 %copy.12 = bf16[384,8,24,256]{3,2,1,0:T(8,128)(2,1)} copy(bf16[384,8,24,256]{3,1,2,0:T(8,128)(2,1)} %bitcast.36) | data formatting | bytes 75497472
  (32 shorter events, 13.5 us)
Async XLA Ops:
  7.2 132.0 %copy-start = (bf16[512,512]{1,0:T(8,128)(2,1)S(1)}, bf16[512,512]{1,0:T(8,128)(2,1)}, u32[]{:S(2)}) copy-start(bf16[512,512]{1,0:T(8,128)(2,1)} %param.4) | copy-start | bytes 1572868
  7.2 78.7 %all-gather.21.cloned.1.call-start = ((), (), s32[]{:S(2)}) async-start(), calls=%async_computation.4 | async-start | bytes 7864320 | tf_op jit(solution)/shard_map/all_gather | solution.py:9
  36.6 97.2 %all-gather.23.cloned.1.call-start = ((), (), s32[]{:S(2)}) async-start(), calls=%async_computation.5 | async-start | bytes 7864320 | tf_op jit(solution)/shard_map/all_gather | solution.py:9
  37.4 588.5 %all-gather.13.cloned.1.call-start = ((), (), s32[]{:S(2)}) async-start(), calls=%async_computation | async-start | bytes 28311552 | tf_op jit(solution)/shard_map/all_gather | solution.py:9
  145.2 962.4 %all-gather.15.cloned.1.call-start = ((), (), s32[]{:S(2)}) async-start(), calls=%async_computation.1 | async-start | bytes 28311552 | tf_op jit(solution)/shard_map/all_gather | solution.py:9
  145.8 1063.1 %all-gather.25.cloned.1.call-start = ((), (), s32[]{:S(2)}) async-start(), calls=%async_computation.6 | async-start | bytes 7864320 | tf_op jit(solution)/shard_map/all_gather | solution.py:9
  1122.9 3.7 copy-start.2
  1162.4 94.3 %all-gather.27.cloned.1.call-start = ((), (), s32[]{:S(2)}) async-start(), calls=%async_computation.7 | async-start | bytes 7864320 | tf_op jit(solution)/shard_map/all_gather | solution.py:9
  1163.0 585.7 %all-gather.17.cloned.1.call-start = ((), (), s32[]{:S(2)}) async-start(), calls=%async_computation.2 | async-start | bytes 28311552 | tf_op jit(solution)/shard_map/all_gather | solution.py:9
  1256.7 5.3 copy-start.3
  1268.1 962.6 %all-gather.19.cloned.1.call-start = ((), (), s32[]{:S(2)}) async-start(), calls=%async_computation.3 | async-start | bytes 28311552 | tf_op jit(solution)/shard_map/all_gather | solution.py:9
  2287.9 25.5 %copy-start.1 = (bf16[512,512]{1,0:T(8,128)(2,1)S(1)}, bf16[512,512]{1,0:T(8,128)(2,1)}, u32[]{:S(2)}) copy-start(bf16[512,512]{1,0:T(8,128)(2,1)} %param.4) | copy-start | bytes 1572868
Sparse Core Ops, SparseCore 0:
  36.8 49.0 all-gather.20
  87.4 46.3 all-gather.22
  145.4 480.4 all-gather.12
  627.2 480.3 all-gather.14
  1162.5 46.3 all-gather.24
  1210.3 46.3 all-gather.26
  1268.2 480.4 all-gather.16
  1750.2 480.3 all-gather.18
